TPU v7x, 32 devices: a whole 2x2x4 slice. The times are simulated.
32 devices in a mesh: sym: 4 (over y, x), row: 8 (over z, core).
Axes of the slice: x: 2, y: 2, z: 4, core: 2. Of those that a mesh axis runs over, the one named last changes fastest.
Arguments:
- psi_inner: bfloat16 [4, 6144, 128], P('sym', 'row'), may hold values from -6 to 6
- outer_state: bfloat16 [512, 128, 128], P('sym', 'row'), may hold values from -6 to 6
- hamiltonian: bfloat16 [4, 6144, 6144], P('sym', 'row'), may hold values from -0.078125 to 0.078125
- dipole_up: bfloat16 [4, 6144, 6144], P('sym', 'row'), may hold values from -0.078125 to 0.078125
- dipole_down: bfloat16 [4, 6144, 6144], P('sym', 'row'), may hold values from -0.078125 to 0.078125
- surface_amp: bfloat16 [4, 6144, 512], P('sym', 'row'), may hold values from -0.078125 to 0.078125
- channel_energy: float32 [512], P('sym'), may hold values from 0.2 to 2
- coupling: bfloat16 [512, 128], P('sym'), may hold values from -0.5 to 0.5
- field: float32 [64], replicated, may hold values from 0.5 to 1.5
- channel_sym: int32 [512, 1], replicated, may hold values from 0 to 3; in each aligned block of 128 rows (0 to 127, 128 to 255, ...) at most 48 rows name the same one
Outputs:
- psi_next: bfloat16 [4, 6144, 128], P('sym', 'row')
- outer_next: bfloat16 [512, 128, 128], P('sym', 'row')
Inputs may be any that keep to these rules, and one draw needn't show every extreme that they name: `channel_sym`: in each aligned block of 128 channels (one sector) at most 48 channels belong to one symmetry, and exactly 48 do in some sector; every symmetry owns some channel.
All inputs are finite; a program needn't handle non-finite values.
Results may differ from a plain program's by a relative error of at most 0.006.
Values may be sent and summed in bfloat16 or wider, within the bound.
No kernel may reach another device: no remote copies, remote signals or barrier semaphores. Data moves between devices by JAX's collectives and lax.ppermute only.
A program may use at most 128 MiB of HBM per device.

v0:
```python
import jax
import jax.numpy as jnp
from jax import lax
from jax.sharding import PartitionSpec as P

BASIS = 6144
SECTOR_CH = 128


STEP_DT = 0.5
ETA_PEAK = 2.0


def padded_2(value, sides, width):
    for axis, dim in sides:
        devices, length = (lax.axis_size(axis), value.shape[dim])
        up = [(i, (i + 1) % devices) for i in range(devices - 1)]
        down = [(j, i) for i, j in up]
        last = lax.slice_in_dim(value, length - width, length, axis=dim)
        initial = lax.slice_in_dim(value, 0, width, axis=dim)
        before = lax.ppermute(last, axis, up)
        after = lax.ppermute(initial, axis, down)
        value = jnp.concatenate([before, value, after], axis=dim)
    return value


def rotate(values, step_scale):
    half_width = values.shape[-1] // 2
    return step_scale * jnp.concatenate(
        [values[..., half_width:], -values[..., :half_width]], axis=-1
    )


def taylor_term(
    psi_rows,
    outer_block,
    hamiltonian,
    dipole_up,
    dipole_down,
    surface_amp,
    channel_energy,
    coupling,
    field,
    channel_sym,
    step_scale,
):
    sym_index = lax.axis_index("sym")
    row_index = lax.axis_index("row")
    sector_ch = outer_block.shape[0]
    points_dev = outer_block.shape[1]
    width = psi_rows.shape[1]
    field_cols = jnp.concatenate([field, field])
    matrices = (hamiltonian[0], dipole_up[0], dipole_down[0])
    block_rows = lax.all_gather(psi_rows, "row", axis=0, tiled=True)
    diagonal_part, raised, lowered = tuple(
        (jnp.dot(matrix, block_rows, preferred_element_type=jnp.float32) for matrix in matrices)
    )
    stacked = jnp.stack([lowered, raised])
    neighbours = padded_2(stacked, (("sym", 0),), 1)
    coupled = neighbours[0] + neighbours[3]
    amplitudes = surface_amp[0]
    member = (channel_sym[:, 0] == sym_index).astype(jnp.float32)
    partial_proj = member[:, None] * lax.dot_general(
        amplitudes, psi_rows, (((0,), (0,)), ((), ())), preferred_element_type=jnp.float32
    )
    edge_rows = outer_block[:, 0, :]
    placed = jnp.where(row_index == 0, edge_rows.astype(jnp.float32), 0.0)
    edge_full = lax.dynamic_update_slice_in_dim(
        jnp.zeros_like(partial_proj), placed, sym_index * sector_ch, 0
    )
    boundary, edge_values = lax.psum((partial_proj, edge_full), ("sym", "row"))
    mismatch = member[:, None] * (edge_values - boundary)
    boundary_sector = lax.dynamic_slice_in_dim(boundary, sym_index * sector_ch, sector_ch, 0)
    surf_scale = (BASIS / SECTOR_CH) ** 0.5
    source = jnp.dot(amplitudes.astype(jnp.float32), mismatch, precision=lax.Precision.HIGHEST)
    inner_h = diagonal_part + field_cols * coupled + surf_scale * source
    inner_next = rotate(inner_h, step_scale)
    radial_ext = padded_2(outer_block, (("row", 1),), 1)
    values = outer_block.astype(jnp.float32)
    lower_ghost = jnp.where(
        row_index == 0, boundary_sector[:, None, :], radial_ext[:, :1, :].astype(jnp.float32)
    )
    upper_ghost = radial_ext[:, -1:, :].astype(jnp.float32)
    padded = jnp.concatenate([lower_ghost, values, upper_ghost], axis=1)
    laplace = padded[:, 2:] - 2.0 * values + padded[:, :-2]
    channel_mix = jnp.dot(
        coupling,
        outer_block.reshape(sector_ch, points_dev * width),
        preferred_element_type=jnp.float32,
    ).reshape(sector_ch, points_dev, width)
    outer_ham = -0.5 * laplace + channel_energy[:, None, None] * values + field_cols * channel_mix
    total_points = points_dev * lax.axis_size("row")
    points = row_index * points_dev + jnp.arange(points_dev, dtype=jnp.int32)
    start_abs = 3 * total_points // 4
    absorb_ramp = jnp.maximum(points - start_abs, 0).astype(jnp.float32) / (
        total_points - start_abs
    )
    absorb = ETA_PEAK * absorb_ramp * absorb_ramp
    outer_next = rotate(outer_ham, step_scale) - step_scale * absorb[None, :, None] * values
    return (inner_next, outer_next)


def on_device(
    psi_inner,
    outer_state,
    hamiltonian,
    dipole_up,
    dipole_down,
    surface_amp,
    channel_energy,
    coupling,
    field,
    channel_sym,
):
    first_inner, first_outer = taylor_term(
        psi_inner[0],
        outer_state,
        hamiltonian,
        dipole_up,
        dipole_down,
        surface_amp,
        channel_energy,
        coupling,
        field,
        channel_sym,
        STEP_DT,
    )
    first_inner = first_inner.astype(jnp.bfloat16)
    first_outer = first_outer.astype(jnp.bfloat16)
    second_inner, second_outer = taylor_term(
        first_inner,
        first_outer,
        hamiltonian,
        dipole_up,
        dipole_down,
        surface_amp,
        channel_energy,
        coupling,
        field,
        channel_sym,
        0.5 * STEP_DT,
    )
    psi_next = (
        psi_inner[0].astype(jnp.float32) + first_inner.astype(jnp.float32) + second_inner
    ).astype(jnp.bfloat16)
    outer_next = (
        outer_state.astype(jnp.float32) + first_outer.astype(jnp.float32) + second_outer
    ).astype(jnp.bfloat16)
    return (psi_next[None], outer_next)


def solution(mesh):
    return jax.shard_map(
        on_device,
        mesh=mesh,
        in_specs=(
            P("sym", "row", None),
            P("sym", "row", None),
            P("sym", "row", None),
            P("sym", "row", None),
            P("sym", "row", None),
            P("sym", "row", None),
            P("sym"),
            P("sym", None),
            P(),
            P(),
        ),
        out_specs=(P("sym", "row", None), P("sym", "row", None)),
        check_vma=False,
    )
```

profile of v0, /device:TPU:0, one launch (start us, length us, event | category | flops | bytes accessed | tf_op | source)
XLA Modules:
  0.0 369.4 jit_solution(8970833456130338308)
XLA Ops:
  8.1 1.3 copy_convert_fusion
  10.1 2.1 convolution_multiply_fusion.4
  13.5 2.4 collective-permute-start.5
  15.9 1.3 collective-permute-start.4
  18.1 1.2 copy.47
  19.5 1.7 collective-permute-done.4
  21.2 132.7 %all-reduce.7.cloned.1.call-done = (f32[512,128]{1,0:T(8,128)}, f32[512,128]{1,0:T(8,128)}) async-done(((f32[512,128]{1,0:T(8,128)}, f32[512,128]{1,0:T(8,128)}), (f32[512,128]{1,0:T(8,128)}, f32[512,128]{1,0:T(8,128)})) %all-reduce.7.cloned.1.call-update) | async-done | bytes 524304 | tf_op jit(solution)/shard_map/psum | solution.py:71
  154.0 0.8 bitcast_select_fusion.1
  154.8 1.1 fusion.15
  157.0 7.5 %fusion.19 = f32[1,768,128]{1,2,0:T(8,128)S(1)} fusion(bf16[1,6144,128]{2,1,0:T(8,128)(2,1)} %all-gather.6.cloned.1.call-done, bf16[1,768,6144]{2,1,0:T(8,128)(2,1)} %param.13), kind=kOutput, calls=%fused_computation.18 | convolution fusion | flops 1207959552 | bytes 11403264 | tf_op jit(solution)/shard_map/dot_general | solution.py:56
  164.5 3.5 collective-permute-start
  168.0 6.9 %fusion.27 = f32[1,768,128]{1,2,0:T(8,128)S(1)} fusion(bf16[1,6144,128]{2,1,0:T(8,128)(2,1)S(1)} %copy-done.1, bf16[1,768,6144]{2,1,0:T(8,128)(2,1)} %param.14), kind=kOutput, calls=%fused_computation.20 | convolution fusion | flops 1207959552 | bytes 11403264 | tf_op jit(solution)/shard_map/dot_general | solution.py:56
  175.0 1.4 collective-permute-start.1
  176.5 3.3 fusion.10
  179.8 7.0 %collective-permute-done.1 = f32[1,768,128]{1,2,0:T(8,128)S(1)} collective-permute-done((f32[1,768,128]{1,2,0:T(8,128)S(1)}, f32[1,768,128]{1,2,0:T(8,128)S(1)}, u32[]{:S(2)}, u32[]{:S(2)}) %collective-permute-start.1) | collective-permute-done | bytes 393248 | tf_op jit(solution)/shard_map/ppermute | solution.py:22
  186.8 1.1 fusion.63
  188.7 1.2 fusion.37
  192.2 1.3 collective-permute-start.7
  193.5 1.3 collective-permute-start.6
  194.8 1.3 fusion.88
  196.1 2.5 copy.33
  198.7 126.8 %all-reduce.5.cloned.1.call-done = (f32[512,128]{1,0:T(8,128)}, f32[512,128]{1,0:T(8,128)}) async-done(((f32[512,128]{1,0:T(8,128)}, f32[512,128]{1,0:T(8,128)}), (f32[512,128]{1,0:T(8,128)}, f32[512,128]{1,0:T(8,128)})) %all-reduce.5.cloned.1.call-update) | async-done | bytes 524304 | tf_op jit(solution)/shard_map/psum | solution.py:71
  325.5 0.8 bitcast_select_fusion
  326.4 1.5 fusion.41
  328.9 1.1 copy.35
  330.0 7.5 %fusion.24 = f32[1,768,128]{1,2,0:T(8,128)S(1)} fusion(bf16[6144,128]{0,1:T(8,128)(2,1)} %all-gather.4.cloned.1.call-done, bf16[1,768,6144]{2,1,0:T(8,128)(2,1)} %param.13), kind=kOutput, calls=%fused_computation.19 | convolution fusion | flops 1207959552 | bytes 11403264 | tf_op jit(solution)/shard_map/dot_general | solution.py:56
  337.6 3.5 collective-permute-start.2
  341.1 6.9 %fusion.32 = f32[1,768,128]{1,2,0:T(8,128)S(1)} fusion(bf16[6144,128]{0,1:T(8,128)(2,1)S(1)} %copy-done.2, bf16[1,768,6144]{2,1,0:T(8,128)(2,1)} %param.14), kind=kOutput, calls=%fused_computation.21 | convolution fusion | flops 1207959552 | bytes 11403264 | tf_op jit(solution)/shard_map/dot_general | solution.py:56
  348.1 1.4 collective-permute-start.3
  349.6 3.2 fusion.16
  352.8 7.0 %collective-permute-done.3 = f32[1,768,128]{1,2,0:T(8,128)S(1)} collective-permute-done((f32[1,768,128]{1,2,0:T(8,128)S(1)}, f32[1,768,128]{1,2,0:T(8,128)S(1)}, u32[]{:S(2)}, u32[]{:S(2)}) %collective-permute-start.3) | collective-permute-done | bytes 393248 | tf_op jit(solution)/shard_map/ppermute | solution.py:22
  359.9 1.1 fusion.61
  (87 shorter events, 9.2 us)
Async XLA Ops:
  8.0 148.3 %copy-start.3 = (bf16[128,16,128]{2,1,0:T(8,128)(2,1)S(1)}, bf16[128,16,128]{2,1,0:T(8,128)(2,1)}, u32[]{:S(2)}) copy-start(bf16[128,16,128]{2,1,0:T(8,128)(2,1)} %param.11) | copy-start | bytes 1572868
  8.0 145.9 %all-reduce.7.cloned.1.call-start = ((), (), s32[]{:S(2)}) async-start(), calls=%async_computation.3 | async-start | bytes 1048576 | tf_op jit(solution)/shard_map/psum | solution.py:71
  12.9 144.1 %all-gather.6.cloned.1.call-start = ((), (), s32[]{:S(2)}) async-start(), calls=%async_computation.1 | async-start | bytes 1769472 | tf_op jit(solution)/shard_map/all_gather | solution.py:54
  13.5 312.0 %all-reduce.5.cloned.1.call-start = ((), (), s32[]{:S(2)}) async-start(), calls=%async_computation.2 | async-start | bytes 1048576 | tf_op jit(solution)/shard_map/psum | solution.py:71
  13.5 7.7 %collective-permute-start.5 = (bf16[128,1,128]{2,0,1:T(8,128)(2,1)S(1)}, bf16[128,1,128]{2,0,1:T(8,128)(2,1)S(1)}, u32[]{:S(2)}, u32[]{:S(2)}) collective-permute-start(bf16[128,1,128]{2,0,1:T(8,128)(2,1)S(1)} %get-tuple-element.19), channel_id=1, source_target_pairs={{0,1},{1,2},{2,3},{3,4},{4,5},{5,6},{6,7},{8,9},{9,10},{10,11},{11... | collective-permute-start | bytes 98312 | tf_op jit(solution)/shard_map/ppermute | solution.py:21
  15.9 5.3 %collective-permute-start.4 = (bf16[128,1,128]{2,0,1:T(8,128)(2,1)S(1)}, bf16[128,1,128]{2,0,1:T(8,128)(2,1)S(1)}, u32[]{:S(2)}, u32[]{:S(2)}) collective-permute-start(bf16[128,1,128]{2,0,1:T(8,128)(2,1)S(1)} %get-tuple-element.18), channel_id=1, source_target_pairs={{1,0},{2,1},{3,2},{4,3},{5,4},{6,5},{7,6},{9,8},{10,9},{11,10},{12... | collective-permute-start | bytes 98312 | tf_op jit(solution)/shard_map/ppermute | solution.py:22
  156.9 18.1 %copy-start.6 = (f32[512,128]{1,0:T(8,128)}, f32[512,128]{1,0:T(8,128)S(1)}, u32[]{:S(2)}) copy-start(f32[512,128]{1,0:T(8,128)S(1)} %bitcast_dynamic-update-slice_fusion) | copy-start | bytes 786436
  157.0 11.1 %copy-start.1 = (bf16[1,6144,128]{2,1,0:T(8,128)(2,1)S(1)}, bf16[1,6144,128]{2,1,0:T(8,128)(2,1)}, u32[]{:S(2)}) copy-start(bf16[1,6144,128]{2,1,0:T(8,128)(2,1)} %all-gather.6.cloned.1.call-done) | copy-start | bytes 4718596
  157.0 19.5 %slice-start = ((s8[9437184]{0:T(1024)(128)(4,1)}), s8[4194304]{0:T(1024)(128)(4,1)S(1)}, s32[]{:S(2)}) async-start(s8[9437184]{0:T(1024)(128)(4,1)} %bitcast.127), calls=%async_computation.4 | async-start | bytes 8388608
  157.0 19.5 %slice-start.1 = ((s8[9437184]{0:T(1024)(128)(4,1)}), s8[4194304]{0:T(1024)(128)(4,1)S(1)}, s32[]{:S(2)}) async-start(s8[9437184]{0:T(1024)(128)(4,1)} %bitcast.127), calls=%async_computation.5 | async-start | bytes 8388608
  164.5 12.0 %slice-start.2 = ((s8[9437184]{0:T(1024)(128)(4,1)}), s8[1048576]{0:T(1024)(128)(4,1)S(1)}, s32[]{:S(2)}) async-start(s8[9437184]{0:T(1024)(128)(4,1)} %bitcast.127), calls=%async_computation.6 | async-start | bytes 2097152
  164.5 15.3 %collective-permute-start = (f32[1,768,128]{1,2,0:T(8,128)S(1)}, f32[1,768,128]{1,2,0:T(8,128)S(1)}, u32[]{:S(2)}, u32[]{:S(2)}) collective-permute-start(f32[1,768,128]{1,2,0:T(8,128)S(1)} %fusion.19), channel_id=1, source_target_pairs={{0,8},{8,16},{16,24},{1,9},{9,17},{17,25},{2,10},{10,18},{18,26},{... | collective-permute-start | bytes 1179656 | tf_op jit(solution)/shard_map/ppermute | solution.py:21
  175.0 11.8 %copy-start.11 = (f32[512,128]{1,0:T(8,128)S(1)}, f32[512,128]{1,0:T(8,128)}, u32[]{:S(2)}) copy-start(f32[512,128]{1,0:T(8,128)} %get-tuple-element.9) | copy-start | bytes 786436
  175.0 11.8 %copy-start.13 = (f32[512,128]{1,0:T(8,128)S(1)}, f32[512,128]{1,0:T(8,128)}, u32[]{:S(2)}) copy-start(f32[512,128]{1,0:T(8,128)} %get-tuple-element.8) | copy-start | bytes 786436
  175.0 15.5 %copy-start.4 = (bf16[1,768,128]{2,1,0:T(8,128)(2,1)S(1)}, bf16[1,768,128]{2,1,0:T(8,128)(2,1)}, u32[]{:S(2)}) copy-start(bf16[1,768,128]{2,1,0:T(8,128)(2,1)} %param.10) | copy-start | bytes 589828
  175.0 11.8 %collective-permute-start.1 = (f32[1,768,128]{1,2,0:T(8,128)S(1)}, f32[1,768,128]{1,2,0:T(8,128)S(1)}, u32[]{:S(2)}, u32[]{:S(2)}) collective-permute-start(f32[1,768,128]{1,2,0:T(8,128)S(1)} %fusion.27), channel_id=1, source_target_pairs={{8,0},{16,8},{24,16},{9,1},{17,9},{25,17},{10,2},{18,10},{26,18},{... | collective-permute-start | bytes 1179656 | tf_op jit(solution)/shard_map/ppermute | solution.py:22
  176.5 18.3 %copy-start.15 = (bf16[128,128]{1,0:T(8,128)(2,1)S(1)}, bf16[128,128]{1,0:T(8,128)(2,1)}, u32[]{:S(2)}) copy-start(bf16[128,128]{1,0:T(8,128)(2,1)} %param.17) | copy-start | bytes 98308
  179.8 146.6 %copy-start.16 = (f32[128]{0:T(128)S(1)}, f32[128]{0:T(128)}, u32[]{:S(2)}) copy-start(f32[128]{0:T(128)} %param.16) | copy-start | bytes 1540
  189.9 140.1 %all-gather.4.cloned.1.call-start = ((), (), s32[]{:S(2)}) async-start(), calls=%async_computation | async-start | bytes 1769472 | tf_op jit(solution)/shard_map/all_gather | solution.py:54
  192.2 6.4 %collective-permute-start.7 = (bf16[128,1,128]{2,0,1:T(8,128)(2,1)S(1)}, bf16[128,1,128]{2,0,1:T(8,128)(2,1)S(1)}, u32[]{:S(2)}, u32[]{:S(2)}) collective-permute-start(bf16[128,1,128]{2,0,1:T(8,128)(2,1)S(1)} %get-tuple-element.17), channel_id=1, source_target_pairs={{0,1},{1,2},{2,3},{3,4},{4,5},{5,6},{6,7},{8,9},{9,10},{10,11},{11... | collective-permute-start | bytes 98312 | tf_op jit(solution)/shard_map/ppermute | solution.py:21
  193.5 5.1 %collective-permute-start.6 = (bf16[128,1,128]{2,0,1:T(8,128)(2,1)}, bf16[128,1,128]{2,0,1:T(8,128)(2,1)S(1)}, u32[]{:S(2)}, u32[]{:S(2)}) collective-permute-start(bf16[128,1,128]{2,0,1:T(8,128)(2,1)} %get-tuple-element.16), channel_id=1, source_target_pairs={{1,0},{2,1},{3,2},{4,3},{5,4},{6,5},{7,6},{9,8},{10,9},{11,10},{12... | collective-permute-start | bytes 98312 | tf_op jit(solution)/shard_map/ppermute | solution.py:22
  330.0 11.1 %copy-start.2 = (bf16[6144,128]{0,1:T(8,128)(2,1)S(1)}, bf16[6144,128]{0,1:T(8,128)(2,1)}, u32[]{:S(2)}) copy-start(bf16[6144,128]{0,1:T(8,128)(2,1)} %all-gather.4.cloned.1.call-done) | copy-start | bytes 4718596
  330.0 19.5 %slice-start.3 = ((s8[9437184]{0:T(1024)(128)(4,1)}), s8[4194304]{0:T(1024)(128)(4,1)S(1)}, s32[]{:S(2)}) async-start(s8[9437184]{0:T(1024)(128)(4,1)} %bitcast.129), calls=%async_computation.7 | async-start | bytes 8388608
  330.0 19.5 %slice-start.4 = ((s8[9437184]{0:T(1024)(128)(4,1)}), s8[4194304]{0:T(1024)(128)(4,1)S(1)}, s32[]{:S(2)}) async-start(s8[9437184]{0:T(1024)(128)(4,1)} %bitcast.129), calls=%async_computation.8 | async-start | bytes 8388608
  337.6 12.0 %slice-start.5 = ((s8[9437184]{0:T(1024)(128)(4,1)}), s8[1048576]{0:T(1024)(128)(4,1)S(1)}, s32[]{:S(2)}) async-start(s8[9437184]{0:T(1024)(128)(4,1)} %bitcast.129), calls=%async_computation.9 | async-start | bytes 2097152
  337.6 22.3 %copy-start.12 = (f32[512,128]{1,0:T(8,128)S(1)}, f32[512,128]{1,0:T(8,128)}, u32[]{:S(2)}) copy-start(f32[512,128]{1,0:T(8,128)} %get-tuple-element.7) | copy-start | bytes 786436
  337.6 22.3 %copy-start.14 = (f32[512,128]{1,0:T(8,128)S(1)}, f32[512,128]{1,0:T(8,128)}, u32[]{:S(2)}) copy-start(f32[512,128]{1,0:T(8,128)} %get-tuple-element.6) | copy-start | bytes 786436
  337.6 15.2 %collective-permute-start.2 = (f32[1,768,128]{1,2,0:T(8,128)S(1)}, f32[1,768,128]{1,2,0:T(8,128)S(1)}, u32[]{:S(2)}, u32[]{:S(2)}) collective-permute-start(f32[1,768,128]{1,2,0:T(8,128)S(1)} %fusion.24), channel_id=1, source_target_pairs={{0,8},{8,16},{16,24},{1,9},{9,17},{17,25},{2,10},{10,18},{18,26},{... | collective-permute-start | bytes 1179656 | tf_op jit(solution)/shard_map/ppermute | solution.py:21
  348.1 12.9 %copy-start.8 = (f32[1,768,64]{1,2,0:T(8,128)S(1)}, f32[1,768,64]{1,2,0:T(8,128)}, u32[]{:S(2)}) copy-start(f32[1,768,64]{1,2,0:T(8,128)} %get-tuple-element.22) | copy-start | bytes 589828
  348.1 12.9 %copy-start.9 = (f32[1,768,64]{1,2,0:T(8,128)S(1)}, f32[1,768,64]{1,2,0:T(8,128)}, u32[]{:S(2)}) copy-start(f32[1,768,64]{1,2,0:T(8,128)} %get-tuple-element.23) | copy-start | bytes 589828
  348.1 12.9 %copy-start.10 = (bf16[1,768,128]{1,2,0:T(8,128)(2,1)S(1)}, bf16[1,768,128]{1,2,0:T(8,128)(2,1)}, u32[]{:S(2)}) copy-start(bf16[1,768,128]{1,2,0:T(8,128)(2,1)} %copy.23) | copy-start | bytes 589828
  348.1 11.8 %collective-permute-start.3 = (f32[1,768,128]{1,2,0:T(8,128)S(1)}, f32[1,768,128]{1,2,0:T(8,128)S(1)}, u32[]{:S(2)}, u32[]{:S(2)}) collective-permute-start(f32[1,768,128]{1,2,0:T(8,128)S(1)} %fusion.32), channel_id=1, source_target_pairs={{8,0},{16,8},{24,16},{9,1},{17,9},{25,17},{10,2},{18,10},{26,18},{... | collective-permute-start | bytes 1179656 | tf_op jit(solution)/shard_map/ppermute | solution.py:22
  (3 other events, 4.2 us)
Sparse Core Ops, SparseCore 0:
  14.9 139.0 all-reduce.6
  190.0 135.4 all-reduce.4
Sparse Core Ops, SparseCore 1:
  15.0 28.6 all-gather.5
  192.0 25.0 all-gather.3
where the time goes:
time: 370 us; the launch traced here: 369 us
  waiting for transfers between devices  276 us (75%)
  matrix products  43.1 us (12%)
  starting transfers between devices  16.5 us (4%)
  between operations  16.1 us (4%)
  other arithmetic  8.83 us (2%)
  local copies, waits for them, and re-layouts  8.52 us (2%)
    psum x2, waiting for transfers between devices, taylor_term(): boundary, edge_values = lax.psum((partial_proj, edge_full), ('sym', 'row'))  260 us
    dot_general x6, matrix products, taylor_term(): jnp.dot(matrix, block_rows, preferred_element_type=jnp.float32)  35.4 us
    ppermute x4, waiting for transfers between devices, padded_2(): after = lax.ppermute(initial, axis, down)  15.8 us
    ppermute x4, starting transfers between devices, padded_2(): before = lax.ppermute(last, axis, up)  10.7 us
  transfers between devices with their start and end apart: 12, of which 5 were waited for; matrix products, arithmetic and copies ran while one was open for 10% of the time, Pallas kernels for 0%

commit v1 on v0

--- a/solution.py
+++ b/solution.py
@@ -1,14 +1,320 @@
 import jax
 import jax.numpy as jnp
 from jax import lax
+from jax.experimental import pallas as pl
+from jax.experimental.pallas import tpu as pltpu
 from jax.sharding import PartitionSpec as P
 
 BASIS = 6144
 SECTOR_CH = 128
-
+CAPACITY = 48
 
 STEP_DT = 0.5
 ETA_PEAK = 2.0
+
+F32 = jnp.float32
+BF16 = jnp.bfloat16
+
+
+def rotate(values, step_scale):
+    half_width = values.shape[-1] // 2
+    return step_scale * jnp.concatenate(
+        [values[..., half_width:], -values[..., :half_width]], axis=-1
+    )
+
+
+def partner(value, axis, mask):
+    count = lax.axis_size(axis)
+    return lax.ppermute(value, axis, [(i, i ^ mask) for i in range(count)])
+
+
+def odd_links(value, axis):
+    count = lax.axis_size(axis)
+    pairs = []
+    for i in range(1, count - 1, 2):
+        pairs += [(i, i + 1), (i + 1, i)]
+    pairs += [(0, count - 1), (count - 1, 0)]
+    return lax.ppermute(value, axis, pairs)
+
+
+def split(value):
+    high = value.astype(BF16)
+    return high, (value - high.astype(F32)).astype(BF16)
+
+
+def partial_kernel(count, first, last, idx_ref, *refs):
+    up_refs = refs[:count]
+    down_refs = refs[count : 2 * count]
+    own_refs = refs[2 * count : 3 * count]
+    vec_refs = refs[3 * count : 4 * count]
+    rest = refs[4 * count :]
+    acc_in = () if first else rest[:3]
+    outs = rest[-3:]
+    sums = []
+    for m, blocks in enumerate((up_refs, down_refs, own_refs)):
+        total = None if first else acc_in[m][...]
+        for block, vec in zip(blocks, vec_refs):
+            term = jnp.dot(block[0], vec[...], preferred_element_type=F32)
+            total = term if total is None else total + term
+        sums.append(total)
+    up, down, own = sums
+    if last:
+        even = idx_ref[idx_ref.shape[0] - 1] == 0
+        outs[0][...] = jnp.where(even, up, down).astype(BF16)
+        outs[1][...] = jnp.where(even, down, up).astype(BF16)
+    else:
+        outs[0][...] = up
+        outs[1][...] = down
+    outs[2][...] = own
+
+
+def partial_products(idx, masks, mats, vecs, acc, last, tile=256):
+    rows = mats[0].shape[1]
+    depth, width = vecs[0].shape
+    count = len(masks)
+    tile = tile if rows % tile == 0 else rows
+    first = acc is None
+
+    def column(mask):
+        return pl.BlockSpec((1, tile, depth), lambda i, ref: (0, i, ref[mask]))
+
+    in_specs = [column(mask) for _ in mats for mask in masks]
+    in_specs += [pl.BlockSpec((depth, width), lambda i, ref: (0, 0)) for _ in vecs]
+    row_spec = pl.BlockSpec((tile, width), lambda i, ref: (i, 0))
+    operands = [m for m in mats for _ in masks] + list(vecs)
+    if not first:
+        in_specs += [row_spec] * 3
+        operands += list(acc)
+    kinds = (BF16, BF16, F32) if last else (F32, F32, F32)
+    size = rows * depth * count * 3
+    return pl.pallas_call(
+        lambda *refs: partial_kernel(count, first, last, *refs),
+        grid_spec=pltpu.PrefetchScalarGridSpec(
+            num_scalar_prefetch=1,
+            grid=(rows // tile,),
+            in_specs=in_specs,
+            out_specs=[row_spec] * 3,
+        ),
+        out_shape=[jax.ShapeDtypeStruct((rows, width), k) for k in kinds],
+        compiler_params=pltpu.CompilerParams(vmem_limit_bytes=24 << 20),
+        cost_estimate=pl.CostEstimate(
+            flops=2 * size * width, bytes_accessed=2 * size, transcendentals=0
+        ),
+        name="products",
+    )(idx, *operands)
+
+
+def combine_kernel(final, scale, step, flag_ref, *refs):
+    own, got_a, got_b, surf, mis_hi, mis_lo, cols = refs[:7]
+    extra = refs[7:-1] if final else refs[7:-2]
+    use_b = (flag_ref[0] != 0).astype(F32)
+    coupled = got_a[...].astype(F32) + use_b * got_b[...].astype(F32)
+    source = jnp.dot(surf[...], mis_hi[...], preferred_element_type=F32)
+    source += jnp.dot(surf[...], mis_lo[...], preferred_element_type=F32)
+    total = own[...] + cols[...] * coupled + scale * source
+    width = total.shape[-1]
+    lane = lax.broadcasted_iota(jnp.int32, total.shape, 1)
+    turned = pltpu.roll(total, width // 2, axis=1)
+    term = jnp.where(lane < width // 2, step, -step) * turned
+    if final:
+        psi, before = extra
+        out = psi[...].astype(F32) + before[...].astype(F32) + term
+        refs[-1][...] = out.astype(BF16)
+    else:
+        term = term.astype(BF16)
+        refs[-2][...] = term
+        refs[-1][...] = lax.dot_general(
+            surf[...], term, (((0,), (0,)), ((), ())), preferred_element_type=F32
+        )
+
+
+def combine(flag, own, got_a, got_b, surf, mismatch, cols, step, scale, extra=()):
+    rows, width = own.shape
+    final = bool(extra)
+    hi, lo = split(mismatch)
+    operands = [own, got_a, got_b, surf, hi, lo, cols, *extra]
+    out_shape = [jax.ShapeDtypeStruct((rows, width), BF16)]
+    if not final:
+        out_shape.append(jax.ShapeDtypeStruct((surf.shape[1], width), F32))
+    vmem = pl.BlockSpec(memory_space=pltpu.VMEM)
+    return pl.pallas_call(
+        lambda *refs: combine_kernel(final, scale, step, *refs),
+        in_specs=[pl.BlockSpec(memory_space=pltpu.SMEM)] + [vmem] * len(operands),
+        out_specs=[vmem] * len(out_shape),
+        out_shape=out_shape,
+        compiler_params=pltpu.CompilerParams(vmem_limit_bytes=16 << 20),
+        cost_estimate=pl.CostEstimate(
+            flops=6 * rows * width * surf.shape[1],
+            bytes_accessed=4 * rows * width * 3,
+            transcendentals=0,
+        ),
+        name="combine",
+    )(flag, *operands)
+
+
+def swapped_step(
+    psi_inner,
+    outer_state,
+    hamiltonian,
+    dipole_up,
+    dipole_down,
+    surface_amp,
+    channel_energy,
+    coupling,
+    field,
+    channel_sym,
+):
+    sym = lax.axis_index("sym").astype(jnp.int32)
+    row = lax.axis_index("row").astype(jnp.int32)
+    syms = lax.axis_size("sym")
+    rows = lax.axis_size("row")
+    psi = psi_inner[0]
+    width = psi.shape[1]
+    sector, points, _ = outer_state.shape
+    slots = syms * CAPACITY
+    scale = (BASIS / SECTOR_CH) ** 0.5
+    field_cols = jnp.concatenate([field, field])
+    cols = field_cols[None, :]
+    mats = (dipole_up, dipole_down, hamiltonian)
+    at_origin = row == 0
+    idx = jnp.concatenate([row ^ jnp.arange(rows, dtype=jnp.int32), (sym & 1)[None]])
+    flag = ((sym > 0) & (sym < syms - 1)).astype(jnp.int32)[None]
+
+    names = channel_sym[:, 0].reshape(syms, sector)
+    lower = (
+        lax.broadcasted_iota(jnp.int32, (sector, sector), 0)
+        < lax.broadcasted_iota(jnp.int32, (sector, sector), 1)
+    )
+    held = (names == sym).astype(F32)
+    rank = jnp.dot(held, lower.astype(F32), preferred_element_type=F32).astype(jnp.int32)
+    block = jnp.arange(syms, dtype=jnp.int32)[:, None] ^ sym
+    slot = jnp.where(names == sym, block * CAPACITY + rank, -1).reshape(-1)
+    pick = (slot[:, None] == jnp.arange(slots, dtype=jnp.int32)[None, :]).astype(BF16)
+    surf = jnp.dot(surface_amp[0], pick, preferred_element_type=F32).astype(BF16)
+
+    mine = lax.dynamic_index_in_dim(names, sym, 0, keepdims=False)
+    same = (mine[:, None] == mine[None, :]).astype(F32)
+    rank_mine = jnp.sum(same * lower.astype(F32), axis=0).astype(jnp.int32)
+    slot_mine = (mine ^ sym) * CAPACITY + rank_mine
+    place = (slot_mine[:, None] == jnp.arange(slots, dtype=jnp.int32)[None, :]).astype(BF16)
+
+    def gather_start(vec):
+        z2 = partner(vec, "row", 4)
+        z1 = partner(vec, "row", 2)
+        c0 = partner(vec, "row", 1)
+        z3 = partner(z2, "row", 2)
+        c1 = partner(z1, "row", 1)
+        c2 = partner(z2, "row", 1)
+        c3 = partner(z3, "row", 1)
+        return {0: vec, 1: c0, 2: z1, 3: c1, 4: z2, 5: c2, 6: z3, 7: c3}
+
+    def products(vecs):
+        acc = partial_products(idx, (0, 1), mats, [vecs[0], vecs[1]], None, False)
+        acc = partial_products(idx, (2, 3, 4, 5), mats, [vecs[k] for k in (2, 3, 4, 5)], acc, False)
+        return partial_products(idx, (6, 7), mats, [vecs[6], vecs[7]], acc, True)
+
+    def row_sum(part):
+        for mask in (4, 2, 1):
+            part = part + partner(part.astype(BF16), "row", mask).astype(F32)
+        return part
+
+    def to_symmetries(stack):
+        blocks = stack.reshape(syms, -1, width)
+        got = [blocks[0]] + [partner(blocks[k], "sym", k) for k in range(1, syms)]
+        return jnp.stack(got)
+
+    vecs = gather_start(psi)
+
+    edge = outer_state[:, 0, :]
+    edge32 = edge.astype(F32)
+    next32 = outer_state[:, 1, :].astype(F32)
+    mix0 = jnp.dot(coupling, edge, preferred_element_type=F32)
+    absorb0 = absorb_of(jnp.zeros((), jnp.int32) + row * points, points * rows)
+    ham0 = -0.5 * (next32 - 2.0 * edge32) + channel_energy[:, None] * edge32 + cols * mix0
+    pre = rotate(ham0, STEP_DT) - STEP_DT * absorb0 * edge32
+    pre_hi, pre_lo = split(pre)
+    packed = jnp.concatenate([edge, pre_hi, pre_lo], axis=1)
+    sorted_edges = lax.dot_general(
+        place, packed, (((0,), (0,)), ((), ())), preferred_element_type=F32
+    ).astype(BF16)
+    sorted_edges = sorted_edges.reshape(syms, CAPACITY, 3, width).transpose(0, 2, 1, 3)
+    arrived = to_symmetries(sorted_edges).reshape(syms, 3, CAPACITY, width)
+    edge_slots = arrived[:, 0].reshape(slots, width).astype(F32)
+    pre_slots = (arrived[:, 1].astype(F32) + arrived[:, 2].astype(F32)).reshape(slots, width)
+
+    part = lax.dot_general(surf, psi, (((0,), (0,)), ((), ())), preferred_element_type=F32)
+    mismatch = row_sum(jnp.where(at_origin, edge_slots, 0.0) - part)
+
+    send_a, send_b, own = products(vecs)
+    got_a = partner(send_a, "sym", 1)
+    got_b = odd_links(send_b, "sym")
+    first, part = combine(flag, own, got_a, got_b, surf, mismatch, cols, STEP_DT, scale)
+
+    vecs = gather_start(first)
+    boundary = edge_slots - mismatch
+    edge_next = (pre_slots + rotate(-0.5 * boundary, STEP_DT)).astype(BF16)
+    mismatch2 = row_sum(jnp.where(at_origin, edge_next.astype(F32), 0.0) - part)
+    boundary2 = edge_next.astype(F32) - mismatch2
+    b_hi, b_lo = split(boundary2)
+    back = jnp.stack(
+        [v.reshape(syms, CAPACITY, width) for v in (edge_next, b_hi, b_lo)], axis=1
+    )
+    back = to_symmetries(back).reshape(syms, 3, CAPACITY, width)
+    back = back.transpose(0, 2, 1, 3).reshape(slots, 3 * width)
+    home = jnp.dot(place, back, preferred_element_type=F32)
+    edge_home = home[:, :width]
+    boundary_home = home[:, width : 2 * width] + home[:, 2 * width :]
+
+    send_a, send_b, own = products(vecs)
+    got_a = partner(send_a, "sym", 1)
+    got_b = odd_links(send_b, "sym")
+    (psi_next,) = combine(
+        flag, own, got_a, got_b, surf, mismatch2, cols, 0.5 * STEP_DT, scale, (psi, first)
+    )
+
+    state = outer_state.transpose(1, 0, 2)
+    ring = [(i, (i + 1) % rows) for i in range(rows)]
+    before = lax.ppermute(state[-2:], "row", ring)
+    after = lax.ppermute(state[:2], "row", [(j, i) for i, j in ring])
+    before = jnp.where(at_origin, jnp.zeros_like(before), before)
+    after = jnp.where(row == rows - 1, jnp.zeros_like(after), after)
+    ext = jnp.concatenate([before, state, after], axis=0)
+    mix = lax.dot_general(ext, coupling, (((1,), (1,)), ((), ())), preferred_element_type=F32)
+    mix = mix.transpose(0, 2, 1)[1:-1]
+    energy = channel_energy[None, :, None]
+    numbers = row * points + jnp.arange(-1, points + 1, dtype=jnp.int32)
+    absorb = absorb_of(numbers, points * rows)[:, None, None]
+    wide = ext.astype(F32)
+    mid = wide[1:-1]
+    ham = -0.5 * (wide[2:] - 2.0 * mid + wide[:-2]) + energy * mid + field_cols * mix
+    outer_first = (rotate(ham, STEP_DT) - STEP_DT * absorb * mid).astype(BF16)
+    outer_first = jnp.concatenate(
+        [
+            outer_first[:1],
+            jnp.where(at_origin, edge_home.astype(BF16), outer_first[1])[None],
+            outer_first[2:-1],
+            jnp.where(row == rows - 1, jnp.zeros_like(outer_first[-1:]), outer_first[-1:]),
+        ],
+        axis=0,
+    )
+    wide = outer_first.astype(F32)
+    wide = jnp.concatenate(
+        [jnp.where(at_origin, boundary_home[None], wide[:1]), wide[1:]], axis=0
+    )
+    mid = wide[1:-1]
+    mix = lax.dot_general(
+        outer_first[1:-1], coupling, (((1,), (1,)), ((), ())), preferred_element_type=F32
+    ).transpose(0, 2, 1)
+    ham = -0.5 * (wide[2:] - 2.0 * mid + wide[:-2]) + energy * mid + field_cols * mix
+    second = rotate(ham, 0.5 * STEP_DT) - 0.5 * STEP_DT * absorb[1:-1] * mid
+    outer_next = (state.astype(F32) + mid + second).astype(BF16).transpose(1, 0, 2)
+    return psi_next[None], outer_next
+
+
+def absorb_of(numbers, total):
+    start = 3 * total // 4
+    ramp = jnp.maximum(numbers - start, 0).astype(F32) / (total - start)
+    return ETA_PEAK * ramp * ramp
 
 
 def padded_2(value, sides, width):
@@ -22,13 +328,6 @@
         after = lax.ppermute(initial, axis, down)
         value = jnp.concatenate([before, value, after], axis=dim)
     return value
-
-
-def rotate(values, step_scale):
-    half_width = values.shape[-1] // 2
-    return step_scale * jnp.concatenate(
-        [values[..., half_width:], -values[..., :half_width]], axis=-1
-    )
 
 
 def taylor_term(
@@ -150,8 +449,9 @@
 
 
 def solution(mesh):
+    quick = mesh.shape["row"] == 8 and mesh.shape["sym"] == 4
     return jax.shard_map(
-        on_device,
+        swapped_step if quick else on_device,
         mesh=mesh,
         in_specs=(
             P("sym", "row", None),

time: 370 us -> 147 us (0.40)
  waiting for transfers between devices: 276 us -> 63.7 us
  matrix products: 43.1 us -> 3.1 us
  Pallas kernels: 0 us -> 30.5 us
  between operations: 16.1 us -> 1.27 us
  local copies, waits for them, and re-layouts: 8.52 us -> 22.8 us
  other arithmetic: 8.83 us -> 4.9 us
  starting transfers between devices: 16.5 us -> 20.4 us
    psum x2 -> x0, waiting for transfers between devices: 260 us -> none  [taylor_term(): boundary, edge_values = lax.psum((partial_proj, edge_full), ('sym', 'row'))]
    ppermute x8 -> x32, waiting for transfers between devices: 15.8 us -> 63.7 us  [the longest x28 50.3 us: partner(): return lax.ppermute(value, axis, [(i, i ^ mask) for i in range(count)])]
    dot_general x12 -> x8, matrix products: 43.1 us -> 3.1 us  [the longest x1 0.91 us: swapped_step(): mix0 = jnp.dot(coupling, edge, preferred_element_type=F32)]
    pallas_call x0 -> x8, Pallas kernels: none -> 30.5 us  [the longest x6 28.7 us: partial_products(): pl.pallas_call(lambda *refs: partial_kernel(count, first, last, *refs), g...]
    unnamed x50 -> x22, local copies, waits for them, and re-layouts: 4.78 us -> 22.1 us
    ppermute x8 -> x32, starting transfers between devices: 16.2 us -> 20.4 us  [the longest x28 16.6 us: partner(): return lax.ppermute(value, axis, [(i, i ^ mask) for i in range(count)])]
  transfers between devices with their start and end apart: 12 -> 32, of which waited for: 5 -> 19; matrix products, arithmetic and copies ran while one was open for 10% -> 8% of each run, Pallas kernels for 0% -> 15%
where the time goes in v1:
time: 147 us
  waiting for transfers between devices  63.7 us (43%)
  Pallas kernels  30.5 us (21%)
  local copies, waits for them, and re-layouts  22.8 us (16%)
  starting transfers between devices  20.4 us (14%)
  other arithmetic  4.9 us (3%)
  matrix products  3.1 us (2%)
    ppermute x28, waiting for transfers between devices, partner(): return lax.ppermute(value, axis, [(i, i ^ mask) for i in range(count)])  50.3 us
    pallas_call x6, Pallas kernels, partial_products(): pl.pallas_call(lambda *refs: partial_kernel(count, first, last, *refs), g...  28.7 us
    unnamed x22, local copies, waits for them, and re-layouts  22.1 us
    ppermute x28, starting transfers between devices, partner(): return lax.ppermute(value, axis, [(i, i ^ mask) for i in range(count)])  16.6 us
    ppermute x2, waiting for transfers between devices, odd_links(): return lax.ppermute(value, axis, pairs)  8.4 us
    ppermute x1, waiting for transfers between devices, swapped_step(): before = lax.ppermute(state[-2:], 'row', ring)  4.92 us
    ppermute x2, starting transfers between devices, odd_links(): return lax.ppermute(value, axis, pairs)  3.74 us
  transfers between devices with their start and end apart: 32, of which 19 were waited for; matrix products, arithmetic and copies ran while one was open for 8% of the time, Pallas kernels for 15%

profile of v1, /device:TPU:0, one launch (start us, length us, event | category | flops | bytes accessed | tf_op | source)
XLA Modules:
  0.0 146.7 jit_solution(16781586249953115045)
XLA Ops:
  0.7 4.1 %collective-permute-start = (bf16[768,128]{1,0:T(8,128)(2,1)}, bf16[768,128]{1,0:T(8,128)(2,1)S(1)}, u32[]{:S(2)}, u32[]{:S(2)}) collective-permute-start(bf16[768,128]{1,0:T(8,128)(2,1)} %bitcast.94), channel_id=1, source_target_pairs={{0,4},{1,5},{2,6},{3,7},{4,0},{5,1},{6,2},{7,3},{8,12},{9,13},{10,... | collective-permute-start | bytes 589832 | tf_op jit(solution)/shard_map/ppermute | solution.py:28
  4.8 1.6 %collective-permute-start.3 = (bf16[768,128]{1,0:T(8,128)(2,1)}, bf16[768,128]{1,0:T(8,128)(2,1)S(1)}, u32[]{:S(2)}, u32[]{:S(2)}) collective-permute-start(bf16[768,128]{1,0:T(8,128)(2,1)} %bitcast.95), channel_id=1, source_target_pairs={{0,2},{1,3},{2,0},{3,1},{4,6},{5,7},{6,4},{7,5},{8,10},{9,11},{10,... | collective-permute-start | bytes 589832 | tf_op jit(solution)/shard_map/ppermute | solution.py:28
  6.4 1.5 copy.58
  10.2 2.5 %collective-permute-start.11 = (bf16[144,128]{1,0:T(8,128)(2,1)S(1)}, bf16[144,128]{1,0:T(8,128)(2,1)S(1)}, u32[]{:S(2)}, u32[]{:S(2)}) collective-permute-start(bf16[144,128]{1,0:T(8,128)(2,1)S(1)} %bitcast.117), channel_id=1, source_target_pairs={{0,24},{8,16},{16,8},{24,0},{1,25},{9,17},{17,9},{25,1},{2,26},{10... | collective-permute-start | bytes 110600 | tf_op jit(solution)/shard_map/ppermute | solution.py:28
  15.2 1.5 %collective-permute-done.10 = bf16[144,128]{1,0:T(8,128)(2,1)S(1)} collective-permute-done((bf16[144,128]{1,0:T(8,128)(2,1)S(1)}, bf16[144,128]{1,0:T(8,128)(2,1)S(1)}, u32[]{:S(2)}, u32[]{:S(2)}) %collective-permute-start.10) | collective-permute-done | bytes 36896 | tf_op jit(solution)/shard_map/ppermute | solution.py:28
  17.9 4.9 %collective-permute-done.27 = bf16[2,128,128]{1,2,0:T(8,128)(2,1)S(1)} collective-permute-done((bf16[2,128,128]{1,2,0:T(8,128)(2,1)S(1)}, bf16[2,128,128]{1,2,0:T(8,128)(2,1)S(1)}, u32[]{:S(2)}, u32[]{:S(2)}) %collective-permute-start.27) | collective-permute-done | bytes 65568 | tf_op jit(solution)/shard_map/ppermute | solution.py:277
  22.9 4.9 %collective-permute-done.12 = bf16[192,128]{1,0:T(8,128)(2,1)S(1)} collective-permute-done((bf16[192,128]{1,0:T(8,128)(2,1)S(1)}, bf16[192,128]{1,0:T(8,128)(2,1)S(1)}, u32[]{:S(2)}, u32[]{:S(2)}) %collective-permute-start.12) | collective-permute-done | bytes 49184 | tf_op jit(solution)/shard_map/ppermute | solution.py:28
  28.3 3.7 %collective-permute-done.13 = bf16[192,128]{1,0:T(8,128)(2,1)S(1)} collective-permute-done((bf16[192,128]{1,0:T(8,128)(2,1)S(1)}, bf16[192,128]{1,0:T(8,128)(2,1)S(1)}, u32[]{:S(2)}, u32[]{:S(2)}) %collective-permute-start.13) | collective-permute-done | bytes 49184 | tf_op jit(solution)/shard_map/ppermute | solution.py:28
  34.5 6.0 %collective-permute-done.1.refs_7_ = bf16[768,128]{1,0:T(8,128)(2,1)S(1)} collective-permute-done((bf16[768,128]{1,0:T(8,128)(2,1)S(1)}, bf16[768,128]{1,0:T(8,128)(2,1)S(1)}, u32[]{:S(2)}, u32[]{:S(2)}) %collective-permute-start.1) | collective-permute-done | bytes 196640 | tf_op jit(solution)/shard_map/ppermute | solution.py:28
  40.5 3.7 %copy-done.1 = bf16[1,768,6144]{2,1,0:T(8,128)(2,1)S(1)} copy-done((bf16[1,768,6144]{2,1,0:T(8,128)(2,1)S(1)}, bf16[1,768,6144]{2,1,0:T(8,128)(2,1)}, u32[]{:S(2)}) %copy-start.1) | copy-done | bytes 9437208
  44.2 3.7 %copy-done.2 = bf16[1,768,6144]{2,1,0:T(8,128)(2,1)S(1)} copy-done((bf16[1,768,6144]{2,1,0:T(8,128)(2,1)S(1)}, bf16[1,768,6144]{2,1,0:T(8,128)(2,1)}, u32[]{:S(2)}) %copy-start.2) | copy-done | bytes 9437208
  47.9 3.7 %copy-done.3 = bf16[1,768,6144]{2,1,0:T(8,128)(2,1)S(1)} copy-done((bf16[1,768,6144]{2,1,0:T(8,128)(2,1)S(1)}, bf16[1,768,6144]{2,1,0:T(8,128)(2,1)}, u32[]{:S(2)}) %copy-start.3) | copy-done | bytes 9437208
  51.5 3.7 %products.6 = (f32[768,128]{1,0:T(8,128)S(1)}, f32[768,128]{1,0:T(8,128)S(1)}, f32[768,128]{1,0:T(8,128)S(1)}) custom-call(s32[9]{0:T(128)S(1)} %pad_add_fusion.refs_0_, bf16[1,768,6144]{2,1,0:T(8,128)(2,1)S(1)} %copy-done.1, bf16[1,768,6144]{2,1,0:T(8,128)(2,1)S(1)} %copy-done.1, bf16[1,768,6144]{2,1,0:T(8,128)(2,1)S(1)} %copy-done.2, ...), custom_call_target="tpu_custom_call" | custom-call | flops 905969664 | bytes 7077888 | tf_op jit(solution)/shard_map/products/pallas_call | solution.py:90
  55.3 7.1 %products.7 = (f32[768,128]{1,0:T(8,128)S(1)}, f32[768,128]{1,0:T(8,128)S(1)}, f32[768,128]{1,0:T(8,128)S(1)}) custom-call(s32[9]{0:T(128)S(1)} %pad_add_fusion.refs_0_, bf16[1,768,6144]{2,1,0:T(8,128)(2,1)S(1)} %copy-done.1, bf16[1,768,6144]{2,1,0:T(8,128)(2,1)S(1)} %copy-done.1, bf16[1,768,6144]{2,1,0:T(8,128)(2,1)S(1)} %copy-done.1, ...), custom_call_target="tpu_custom_call" | custom-call | flops 1811939328 | bytes 14155776 | tf_op jit(solution)/shard_map/products/pallas_call | solution.py:90
  62.4 3.7 %copy-done.4 = bf16[1,768,6144]{2,1,0:T(8,128)(2,1)S(1)} copy-done((bf16[1,768,6144]{2,1,0:T(8,128)(2,1)S(1)}, bf16[1,768,6144]{2,1,0:T(8,128)(2,1)}, u32[]{:S(2)}) %copy-start.4) | copy-done | bytes 9437208
  66.1 3.6 %products.8 = (bf16[768,128]{1,0:T(8,128)(2,1)S(1)}, bf16[768,128]{1,0:T(8,128)(2,1)S(1)}, f32[768,128]{1,0:T(8,128)S(1)}) custom-call(s32[9]{0:T(128)S(1)} %pad_add_fusion.refs_0_, bf16[1,768,6144]{2,1,0:T(8,128)(2,1)S(1)} %copy-done.1, bf16[1,768,6144]{2,1,0:T(8,128)(2,1)S(1)} %copy-done.1, bf16[1,768,6144]{2,1,0:T(8,128)(2,1)S(1)} %copy-done.2, ...), custom_call_target="tpu_custom_call" | custom-call | flops 905969664 | bytes 7077888 | tf_op jit(solution)/shard_map/products/pallas_call | solution.py:90
  70.4 2.4 %collective-permute-start.8 = (bf16[768,128]{1,0:T(8,128)(2,1)S(1)}, bf16[768,128]{1,0:T(8,128)(2,1)S(1)}, u32[]{:S(2)}, u32[]{:S(2)}) collective-permute-start(bf16[768,128]{1,0:T(8,128)(2,1)S(1)} %get-tuple-element.30), channel_id=1, source_target_pairs={{8,16},{16,8},{0,24},{24,0},{9,17},{17,9},{1,25},{25,1},{10,18},{1... | collective-permute-start | bytes 589832 | tf_op jit(solution)/shard_map/ppermute | solution.py:37
  72.8 4.8 %collective-permute-done.7.refs_2_ = bf16[768,128]{1,0:T(8,128)(2,1)S(1)} collective-permute-done((bf16[768,128]{1,0:T(8,128)(2,1)S(1)}, bf16[768,128]{1,0:T(8,128)(2,1)S(1)}, u32[]{:S(2)}, u32[]{:S(2)}) %collective-permute-start.7) | collective-permute-done | bytes 196640 | tf_op jit(solution)/shard_map/ppermute | solution.py:28
  77.6 4.7 %collective-permute-done.8.refs_3_ = bf16[768,128]{1,0:T(8,128)(2,1)S(1)} collective-permute-done((bf16[768,128]{1,0:T(8,128)(2,1)S(1)}, bf16[768,128]{1,0:T(8,128)(2,1)S(1)}, u32[]{:S(2)}, u32[]{:S(2)}) %collective-permute-start.8) | collective-permute-done | bytes 196640 | tf_op jit(solution)/shard_map/ppermute | solution.py:37
  83.5 4.9 %collective-permute-done.24 = bf16[192,128]{1,0:T(8,128)(2,1)S(1)} collective-permute-done((bf16[192,128]{1,0:T(8,128)(2,1)S(1)}, bf16[192,128]{1,0:T(8,128)(2,1)S(1)}, u32[]{:S(2)}, u32[]{:S(2)}) %collective-permute-start.24) | collective-permute-done | bytes 49184 | tf_op jit(solution)/shard_map/ppermute | solution.py:28
  88.7 3.9 %collective-permute-done.25 = bf16[192,128]{1,0:T(8,128)(2,1)S(1)} collective-permute-done((bf16[192,128]{1,0:T(8,128)(2,1)S(1)}, bf16[192,128]{1,0:T(8,128)(2,1)S(1)}, u32[]{:S(2)}, u32[]{:S(2)}) %collective-permute-start.25) | collective-permute-done | bytes 49184 | tf_op jit(solution)/shard_map/ppermute | solution.py:28
  95.2 1.6 %collective-permute-start.30 = (bf16[144,128]{1,0:T(8,128)(2,1)S(1)}, bf16[144,128]{1,0:T(8,128)(2,1)S(1)}, u32[]{:S(2)}, u32[]{:S(2)}) collective-permute-start(bf16[144,128]{1,0:T(8,128)(2,1)S(1)} %bitcast.119), channel_id=1, source_target_pairs={{0,16},{8,24},{16,0},{24,8},{1,17},{9,25},{17,1},{25,9},{2,18},{10... | collective-permute-start | bytes 110600 | tf_op jit(solution)/shard_map/ppermute | solution.py:28
  96.9 1.5 collective-permute-start.29
  102.1 7.1 %collective-permute-done.15.refs_15_ = bf16[768,128]{1,0:T(8,128)(2,1)S(1)} collective-permute-done((bf16[768,128]{1,0:T(8,128)(2,1)S(1)}, bf16[768,128]{1,0:T(8,128)(2,1)S(1)}, u32[]{:S(2)}, u32[]{:S(2)}) %collective-permute-start.15) | collective-permute-done | bytes 196640 | tf_op jit(solution)/shard_map/ppermute | solution.py:28
  109.8 6.2 %collective-permute-done.16.refs_7_ = bf16[768,128]{1,0:T(8,128)(2,1)S(1)} collective-permute-done((bf16[768,128]{1,0:T(8,128)(2,1)S(1)}, bf16[768,128]{1,0:T(8,128)(2,1)S(1)}, u32[]{:S(2)}, u32[]{:S(2)}) %collective-permute-start.16) | collective-permute-done | bytes 196640 | tf_op jit(solution)/shard_map/ppermute | solution.py:28
  116.0 3.6 %products.9 = (f32[768,128]{1,0:T(8,128)S(1)}, f32[768,128]{1,0:T(8,128)S(1)}, f32[768,128]{1,0:T(8,128)S(1)}) custom-call(s32[9]{0:T(128)S(1)} %pad_add_fusion.refs_0_, bf16[1,768,6144]{2,1,0:T(8,128)(2,1)S(1)} %copy-done.1, bf16[1,768,6144]{2,1,0:T(8,128)(2,1)S(1)} %copy-done.1, bf16[1,768,6144]{2,1,0:T(8,128)(2,1)S(1)} %copy-done.2, ...), custom_call_target="tpu_custom_call" | custom-call | flops 905969664 | bytes 7077888 | tf_op jit(solution)/shard_map/products/pallas_call | solution.py:90
  119.6 7.1 %products.10 = (f32[768,128]{1,0:T(8,128)S(1)}, f32[768,128]{1,0:T(8,128)S(1)}, f32[768,128]{1,0:T(8,128)S(1)}) custom-call(s32[9]{0:T(128)S(1)} %pad_add_fusion.refs_0_, bf16[1,768,6144]{2,1,0:T(8,128)(2,1)S(1)} %copy-done.1, bf16[1,768,6144]{2,1,0:T(8,128)(2,1)S(1)} %copy-done.1, bf16[1,768,6144]{2,1,0:T(8,128)(2,1)S(1)} %copy-done.1, ...), custom_call_target="tpu_custom_call" | custom-call | flops 1811939328 | bytes 14155776 | tf_op jit(solution)/shard_map/products/pallas_call | solution.py:90
  126.7 3.7 %copy-done.5 = bf16[1,768,6144]{2,1,0:T(8,128)(2,1)S(1)} copy-done((bf16[1,768,6144]{2,1,0:T(8,128)(2,1)S(1)}, bf16[1,768,6144]{2,1,0:T(8,128)(2,1)}, u32[]{:S(2)}) %copy-start.5) | copy-done | bytes 9437208
  130.4 3.6 %products.11 = (bf16[768,128]{1,0:T(8,128)(2,1)S(1)}, bf16[768,128]{1,0:T(8,128)(2,1)S(1)}, f32[768,128]{1,0:T(8,128)S(1)}) custom-call(s32[9]{0:T(128)S(1)} %pad_add_fusion.refs_0_, bf16[1,768,6144]{2,1,0:T(8,128)(2,1)S(1)} %copy-done.1, bf16[1,768,6144]{2,1,0:T(8,128)(2,1)S(1)} %copy-done.1, bf16[1,768,6144]{2,1,0:T(8,128)(2,1)S(1)} %copy-done.2, ...), custom_call_target="tpu_custom_call" | custom-call | flops 905969664 | bytes 7077888 | tf_op jit(solution)/shard_map/products/pallas_call | solution.py:90
  137.2 2.2 %copy.80 = bf16[128,16,128]{2,1,0:T(8,128)(2,1)} copy(bf16[128,16,128]{0,2,1:T(8,128)(2,1)} %fusion.21) | data formatting | bytes 1048576
  139.4 2.4 %collective-permute-done.22.refs_2_ = bf16[768,128]{1,0:T(8,128)(2,1)S(1)} collective-permute-done((bf16[768,128]{1,0:T(8,128)(2,1)S(1)}, bf16[768,128]{1,0:T(8,128)(2,1)S(1)}, u32[]{:S(2)}, u32[]{:S(2)}) %collective-permute-start.22) | collective-permute-done | bytes 196640 | tf_op jit(solution)/shard_map/ppermute | solution.py:28
  141.9 3.7 %collective-permute-done.23.refs_3_ = bf16[768,128]{1,0:T(8,128)(2,1)S(1)} collective-permute-done((bf16[768,128]{1,0:T(8,128)(2,1)S(1)}, bf16[768,128]{1,0:T(8,128)(2,1)S(1)}, u32[]{:S(2)}, u32[]{:S(2)}) %collective-permute-start.23) | collective-permute-done | bytes 196640 | tf_op jit(solution)/shard_map/ppermute | solution.py:37
  (130 shorter events, 22.1 us)
Async XLA Ops:
  0.7 32.8 %collective-permute-start = (bf16[768,128]{1,0:T(8,128)(2,1)}, bf16[768,128]{1,0:T(8,128)(2,1)S(1)}, u32[]{:S(2)}, u32[]{:S(2)}) collective-permute-start(bf16[768,128]{1,0:T(8,128)(2,1)} %bitcast.94), channel_id=1, source_target_pairs={{0,4},{1,5},{2,6},{3,7},{4,0},{5,1},{6,2},{7,3},{8,12},{9,13},{10,... | collective-permute-start | bytes 589832 | tf_op jit(solution)/shard_map/ppermute | solution.py:28
  4.8 29.0 %collective-permute-start.3 = (bf16[768,128]{1,0:T(8,128)(2,1)}, bf16[768,128]{1,0:T(8,128)(2,1)S(1)}, u32[]{:S(2)}, u32[]{:S(2)}) collective-permute-start(bf16[768,128]{1,0:T(8,128)(2,1)} %bitcast.95), channel_id=1, source_target_pairs={{0,2},{1,3},{2,0},{3,1},{4,6},{5,7},{6,4},{7,5},{8,10},{9,11},{10,... | collective-permute-start | bytes 589832 | tf_op jit(solution)/shard_map/ppermute | solution.py:28
  10.2 5.0 %collective-permute-start.11 = (bf16[144,128]{1,0:T(8,128)(2,1)S(1)}, bf16[144,128]{1,0:T(8,128)(2,1)S(1)}, u32[]{:S(2)}, u32[]{:S(2)}) collective-permute-start(bf16[144,128]{1,0:T(8,128)(2,1)S(1)} %bitcast.117), channel_id=1, source_target_pairs={{0,24},{8,16},{16,8},{24,0},{1,25},{9,17},{17,9},{25,1},{2,26},{10... | collective-permute-start | bytes 110600 | tf_op jit(solution)/shard_map/ppermute | solution.py:28
  12.7 4.0 %collective-permute-start.10 = (bf16[144,128]{1,0:T(8,128)(2,1)S(1)}, bf16[144,128]{1,0:T(8,128)(2,1)S(1)}, u32[]{:S(2)}, u32[]{:S(2)}) collective-permute-start(bf16[144,128]{1,0:T(8,128)(2,1)S(1)} %bitcast.116), channel_id=1, source_target_pairs={{0,16},{8,24},{16,0},{24,8},{1,17},{9,25},{17,1},{25,9},{2,18},{10... | collective-permute-start | bytes 110600 | tf_op jit(solution)/shard_map/ppermute | solution.py:28
  13.3 4.0 %collective-permute-start.9 = (bf16[144,128]{1,0:T(8,128)(2,1)S(1)}, bf16[144,128]{1,0:T(8,128)(2,1)S(1)}, u32[]{:S(2)}, u32[]{:S(2)}) collective-permute-start(bf16[144,128]{1,0:T(8,128)(2,1)S(1)} %bitcast.114), channel_id=1, source_target_pairs={{0,8},{8,0},{16,24},{24,16},{1,9},{9,1},{17,25},{25,17},{2,10},{10... | collective-permute-start | bytes 110600 | tf_op jit(solution)/shard_map/ppermute | solution.py:28
  15.2 25.3 %collective-permute-start.6 = (bf16[768,128]{1,0:T(8,128)(2,1)S(1)}, bf16[768,128]{1,0:T(8,128)(2,1)S(1)}, u32[]{:S(2)}, u32[]{:S(2)}) collective-permute-start(bf16[768,128]{1,0:T(8,128)(2,1)S(1)} %bitcast.96), channel_id=1, source_target_pairs={{0,1},{1,0},{2,3},{3,2},{4,5},{5,4},{6,7},{7,6},{8,9},{9,8},{10,11... | collective-permute-start | bytes 589832 | tf_op jit(solution)/shard_map/ppermute | solution.py:28
  16.8 6.1 %collective-permute-start.28 = (bf16[2,128,128]{1,2,0:T(8,128)(2,1)S(1)}, bf16[2,128,128]{1,2,0:T(8,128)(2,1)S(1)}, u32[]{:S(2)}, u32[]{:S(2)}) collective-permute-start(bf16[2,128,128]{1,2,0:T(8,128)(2,1)S(1)} %get-tuple-element.71), channel_id=1, source_target_pairs={{1,0},{2,1},{3,2},{4,3},{5,4},{6,5},{7,6},{0,7},{9,8},{10,9},{11,1... | collective-permute-start | bytes 196616 | tf_op jit(solution)/shard_map/ppermute | solution.py:278
  17.3 5.5 %collective-permute-start.27 = (bf16[2,128,128]{1,2,0:T(8,128)(2,1)S(1)}, bf16[2,128,128]{1,2,0:T(8,128)(2,1)S(1)}, u32[]{:S(2)}, u32[]{:S(2)}) collective-permute-start(bf16[2,128,128]{1,2,0:T(8,128)(2,1)S(1)} %get-tuple-element.70), channel_id=1, source_target_pairs={{0,1},{1,2},{2,3},{3,4},{4,5},{5,6},{6,7},{7,0},{8,9},{9,10},{10,1... | collective-permute-start | bytes 196616 | tf_op jit(solution)/shard_map/ppermute | solution.py:277
  22.8 5.0 %collective-permute-start.12 = (bf16[192,128]{1,0:T(8,128)(2,1)S(1)}, bf16[192,128]{1,0:T(8,128)(2,1)S(1)}, u32[]{:S(2)}, u32[]{:S(2)}) collective-permute-start(bf16[192,128]{1,0:T(8,128)(2,1)S(1)} %get-tuple-element.87), channel_id=1, source_target_pairs={{0,4},{1,5},{2,6},{3,7},{4,0},{5,1},{6,2},{7,3},{8,12},{9,13},{10,... | collective-permute-start | bytes 147464 | tf_op jit(solution)/shard_map/ppermute | solution.py:28
  27.8 4.2 %collective-permute-start.13 = (bf16[192,128]{1,0:T(8,128)(2,1)S(1)}, bf16[192,128]{1,0:T(8,128)(2,1)S(1)}, u32[]{:S(2)}, u32[]{:S(2)}) collective-permute-start(bf16[192,128]{1,0:T(8,128)(2,1)S(1)} %fusion.39), channel_id=1, source_target_pairs={{0,2},{1,3},{2,0},{3,1},{4,6},{5,7},{6,4},{7,5},{8,10},{9,11},{10,... | collective-permute-start | bytes 147464 | tf_op jit(solution)/shard_map/ppermute | solution.py:28
  32.0 1.3 collective-permute-start.14
  33.4 7.0 %collective-permute-start.1 = (bf16[768,128]{1,0:T(8,128)(2,1)S(1)}, bf16[768,128]{1,0:T(8,128)(2,1)S(1)}, u32[]{:S(2)}, u32[]{:S(2)}) collective-permute-start(bf16[768,128]{1,0:T(8,128)(2,1)S(1)} %collective-permute-done.refs_15_), channel_id=1, source_target_pairs={{0,2},{1,3},{2,0},{3,1},{4,6},{5,7},{6,4},{7,5},{8,10},{9,11},{10,... | collective-permute-start | bytes 589832 | tf_op jit(solution)/shard_map/ppermute | solution.py:28
  33.5 21.8 %collective-permute-start.5 = (bf16[768,128]{1,0:T(8,128)(2,1)S(1)}, bf16[768,128]{1,0:T(8,128)(2,1)S(1)}, u32[]{:S(2)}, u32[]{:S(2)}) collective-permute-start(bf16[768,128]{1,0:T(8,128)(2,1)S(1)} %collective-permute-done.refs_15_), channel_id=1, source_target_pairs={{0,1},{1,0},{2,3},{3,2},{4,5},{5,4},{6,7},{7,6},{8,9},{9,8},{10,11... | collective-permute-start | bytes 589832 | tf_op jit(solution)/shard_map/ppermute | solution.py:28
  33.8 21.5 %collective-permute-start.4 = (bf16[768,128]{1,0:T(8,128)(2,1)S(1)}, bf16[768,128]{1,0:T(8,128)(2,1)S(1)}, u32[]{:S(2)}, u32[]{:S(2)}) collective-permute-start(bf16[768,128]{1,0:T(8,128)(2,1)S(1)} %collective-permute-done.3.refs_13_), channel_id=1, source_target_pairs={{0,1},{1,0},{2,3},{3,2},{4,5},{5,4},{6,7},{7,6},{8,9},{9,8},{10,11... | collective-permute-start | bytes 589832 | tf_op jit(solution)/shard_map/ppermute | solution.py:28
  40.5 21.9 %collective-permute-start.2 = (bf16[768,128]{1,0:T(8,128)(2,1)S(1)}, bf16[768,128]{1,0:T(8,128)(2,1)S(1)}, u32[]{:S(2)}, u32[]{:S(2)}) collective-permute-start(bf16[768,128]{1,0:T(8,128)(2,1)S(1)} %collective-permute-done.1.refs_7_), channel_id=1, source_target_pairs={{0,1},{1,0},{2,3},{3,2},{4,5},{5,4},{6,7},{7,6},{8,9},{9,8},{10,11... | collective-permute-start | bytes 589832 | tf_op jit(solution)/shard_map/ppermute | solution.py:28
  69.7 7.8 %collective-permute-start.7 = (bf16[768,128]{1,0:T(8,128)(2,1)S(1)}, bf16[768,128]{1,0:T(8,128)(2,1)S(1)}, u32[]{:S(2)}, u32[]{:S(2)}) collective-permute-start(bf16[768,128]{1,0:T(8,128)(2,1)S(1)} %get-tuple-element.29), channel_id=1, source_target_pairs={{0,8},{8,0},{16,24},{24,16},{1,9},{9,1},{17,25},{25,17},{2,10},{10... | collective-permute-start | bytes 589832 | tf_op jit(solution)/shard_map/ppermute | solution.py:28
  70.4 11.9 %collective-permute-start.8 = (bf16[768,128]{1,0:T(8,128)(2,1)S(1)}, bf16[768,128]{1,0:T(8,128)(2,1)S(1)}, u32[]{:S(2)}, u32[]{:S(2)}) collective-permute-start(bf16[768,128]{1,0:T(8,128)(2,1)S(1)} %get-tuple-element.30), channel_id=1, source_target_pairs={{8,16},{16,8},{0,24},{24,0},{9,17},{17,9},{1,25},{25,1},{10,18},{1... | collective-permute-start | bytes 589832 | tf_op jit(solution)/shard_map/ppermute | solution.py:37
  83.1 5.3 %collective-permute-start.24 = (bf16[192,128]{1,0:T(8,128)(2,1)S(1)}, bf16[192,128]{1,0:T(8,128)(2,1)S(1)}, u32[]{:S(2)}, u32[]{:S(2)}) collective-permute-start(bf16[192,128]{1,0:T(8,128)(2,1)S(1)} %get-tuple-element.56), channel_id=1, source_target_pairs={{0,4},{1,5},{2,6},{3,7},{4,0},{5,1},{6,2},{7,3},{8,12},{9,13},{10,... | collective-permute-start | bytes 147464 | tf_op jit(solution)/shard_map/ppermute | solution.py:28
  88.4 4.2 %collective-permute-start.25 = (bf16[192,128]{1,0:T(8,128)(2,1)S(1)}, bf16[192,128]{1,0:T(8,128)(2,1)S(1)}, u32[]{:S(2)}, u32[]{:S(2)}) collective-permute-start(bf16[192,128]{1,0:T(8,128)(2,1)S(1)} %fusion.40), channel_id=1, source_target_pairs={{0,2},{1,3},{2,0},{3,1},{4,6},{5,7},{6,4},{7,5},{8,10},{9,11},{10,... | collective-permute-start | bytes 147464 | tf_op jit(solution)/shard_map/ppermute | solution.py:28
  92.6 1.3 collective-permute-start.26
  94.6 5.2 %collective-permute-start.31 = (bf16[144,128]{1,0:T(8,128)(2,1)S(1)}, bf16[144,128]{1,0:T(8,128)(2,1)S(1)}, u32[]{:S(2)}, u32[]{:S(2)}) collective-permute-start(bf16[144,128]{1,0:T(8,128)(2,1)S(1)} %bitcast.123), channel_id=1, source_target_pairs={{0,24},{8,16},{16,8},{24,0},{1,25},{9,17},{17,9},{25,1},{2,26},{10... | collective-permute-start | bytes 110600 | tf_op jit(solution)/shard_map/ppermute | solution.py:28
  95.2 4.6 %collective-permute-start.30 = (bf16[144,128]{1,0:T(8,128)(2,1)S(1)}, bf16[144,128]{1,0:T(8,128)(2,1)S(1)}, u32[]{:S(2)}, u32[]{:S(2)}) collective-permute-start(bf16[144,128]{1,0:T(8,128)(2,1)S(1)} %bitcast.119), channel_id=1, source_target_pairs={{0,16},{8,24},{16,0},{24,8},{1,17},{9,25},{17,1},{25,9},{2,18},{10... | collective-permute-start | bytes 110600 | tf_op jit(solution)/shard_map/ppermute | solution.py:28
  96.9 4.0 %collective-permute-start.29 = (bf16[144,128]{1,0:T(8,128)(2,1)S(1)}, bf16[144,128]{1,0:T(8,128)(2,1)S(1)}, u32[]{:S(2)}, u32[]{:S(2)}) collective-permute-start(bf16[144,128]{1,0:T(8,128)(2,1)S(1)} %bitcast.121), channel_id=1, source_target_pairs={{0,8},{8,0},{16,24},{24,16},{1,9},{9,1},{17,25},{25,17},{2,10},{10... | collective-permute-start | bytes 110600 | tf_op jit(solution)/shard_map/ppermute | solution.py:28
  98.4 10.8 %collective-permute-start.15 = (bf16[768,128]{1,0:T(8,128)(2,1)S(1)}, bf16[768,128]{1,0:T(8,128)(2,1)S(1)}, u32[]{:S(2)}, u32[]{:S(2)}) collective-permute-start(bf16[768,128]{1,0:T(8,128)(2,1)S(1)} %get-tuple-element.31.refs_7_.refs_9_), channel_id=1, source_target_pairs={{0,4},{1,5},{2,6},{3,7},{4,0},{5,1},{6,2},{7,3},{8,12},{9,13},{10,... | collective-permute-start | bytes 589832 | tf_op jit(solution)/shard_map/ppermute | solution.py:28
  98.5 10.7 %collective-permute-start.18 = (bf16[768,128]{1,0:T(8,128)(2,1)S(1)}, bf16[768,128]{1,0:T(8,128)(2,1)S(1)}, u32[]{:S(2)}, u32[]{:S(2)}) collective-permute-start(bf16[768,128]{1,0:T(8,128)(2,1)S(1)} %get-tuple-element.31.refs_7_.refs_9_), channel_id=1, source_target_pairs={{0,2},{1,3},{2,0},{3,1},{4,6},{5,7},{6,4},{7,5},{8,10},{9,11},{10,... | collective-permute-start | bytes 589832 | tf_op jit(solution)/shard_map/ppermute | solution.py:28
  99.8 16.2 %collective-permute-start.21 = (bf16[768,128]{1,0:T(8,128)(2,1)S(1)}, bf16[768,128]{1,0:T(8,128)(2,1)S(1)}, u32[]{:S(2)}, u32[]{:S(2)}) collective-permute-start(bf16[768,128]{1,0:T(8,128)(2,1)S(1)} %get-tuple-element.31.refs_7_.refs_9_), channel_id=1, source_target_pairs={{0,1},{1,0},{2,3},{3,2},{4,5},{5,4},{6,7},{7,6},{8,9},{9,8},{10,11... | collective-permute-start | bytes 589832 | tf_op jit(solution)/shard_map/ppermute | solution.py:28
  109.2 6.8 %collective-permute-start.16 = (bf16[768,128]{1,0:T(8,128)(2,1)S(1)}, bf16[768,128]{1,0:T(8,128)(2,1)S(1)}, u32[]{:S(2)}, u32[]{:S(2)}) collective-permute-start(bf16[768,128]{1,0:T(8,128)(2,1)S(1)} %collective-permute-done.15.refs_15_), channel_id=1, source_target_pairs={{0,2},{1,3},{2,0},{3,1},{4,6},{5,7},{6,4},{7,5},{8,10},{9,11},{10,... | collective-permute-start | bytes 589832 | tf_op jit(solution)/shard_map/ppermute | solution.py:28
  109.2 10.4 %collective-permute-start.20 = (bf16[768,128]{1,0:T(8,128)(2,1)S(1)}, bf16[768,128]{1,0:T(8,128)(2,1)S(1)}, u32[]{:S(2)}, u32[]{:S(2)}) collective-permute-start(bf16[768,128]{1,0:T(8,128)(2,1)S(1)} %collective-permute-done.15.refs_15_), channel_id=1, source_target_pairs={{0,1},{1,0},{2,3},{3,2},{4,5},{5,4},{6,7},{7,6},{8,9},{9,8},{10,11... | collective-permute-start | bytes 589832 | tf_op jit(solution)/shard_map/ppermute | solution.py:28
  109.2 10.4 %collective-permute-start.19 = (bf16[768,128]{1,0:T(8,128)(2,1)S(1)}, bf16[768,128]{1,0:T(8,128)(2,1)S(1)}, u32[]{:S(2)}, u32[]{:S(2)}) collective-permute-start(bf16[768,128]{1,0:T(8,128)(2,1)S(1)} %collective-permute-done.18.refs_13_), channel_id=1, source_target_pairs={{0,1},{1,0},{2,3},{3,2},{4,5},{5,4},{6,7},{7,6},{8,9},{9,8},{10,11... | collective-permute-start | bytes 589832 | tf_op jit(solution)/shard_map/ppermute | solution.py:28
  116.0 10.7 %collective-permute-start.17 = (bf16[768,128]{1,0:T(8,128)(2,1)S(1)}, bf16[768,128]{1,0:T(8,128)(2,1)S(1)}, u32[]{:S(2)}, u32[]{:S(2)}) collective-permute-start(bf16[768,128]{1,0:T(8,128)(2,1)S(1)} %collective-permute-done.16.refs_7_), channel_id=1, source_target_pairs={{0,1},{1,0},{2,3},{3,2},{4,5},{5,4},{6,7},{7,6},{8,9},{9,8},{10,11... | collective-permute-start | bytes 589832 | tf_op jit(solution)/shard_map/ppermute | solution.py:28
  134.0 7.8 %collective-permute-start.22 = (bf16[768,128]{1,0:T(8,128)(2,1)S(1)}, bf16[768,128]{1,0:T(8,128)(2,1)S(1)}, u32[]{:S(2)}, u32[]{:S(2)}) collective-permute-start(bf16[768,128]{1,0:T(8,128)(2,1)S(1)} %get-tuple-element.39), channel_id=1, source_target_pairs={{0,8},{8,0},{16,24},{24,16},{1,9},{9,1},{17,25},{25,17},{2,10},{10... | collective-permute-start | bytes 589832 | tf_op jit(solution)/shard_map/ppermute | solution.py:28
  134.7 10.8 %collective-permute-start.23 = (bf16[768,128]{1,0:T(8,128)(2,1)S(1)}, bf16[768,128]{1,0:T(8,128)(2,1)S(1)}, u32[]{:S(2)}, u32[]{:S(2)}) collective-permute-start(bf16[768,128]{1,0:T(8,128)(2,1)S(1)} %get-tuple-element.40), channel_id=1, source_target_pairs={{8,16},{16,8},{0,24},{24,0},{9,17},{17,9},{1,25},{25,1},{10,18},{1... | collective-permute-start | bytes 589832 | tf_op jit(solution)/shard_map/ppermute | solution.py:37
  (10 other events, 72.7 us)
